TPU v7x, 32 devices: a whole 2x2x4 slice. The times are simulated.
32 devices in a mesh: grp: 8 (over z, x), lane: 4 (over y, core).
Axes of the slice: x: 2, y: 2, z: 4, core: 2. Of those that a mesh axis runs over, the one named last changes fastest.
Arguments:
- features: bfloat16 [65536, 128], P(('grp', 'lane')), may hold values from -600 to 600
- tiles: bfloat16 [512, 7, 128, 128], P(('grp', 'lane')), may hold values from -0.125 to 0.125
- tile_cols: int32 [512, 7], P(('grp', 'lane')), may hold values from 0 to 23
- send_index: int32 [32, 2, 512], P(('grp', 'lane')), may hold values from 0 to 2047
- send_count: int32 [32, 2], P(('grp', 'lane')), may hold values from 128 to 512, as said below
- coef: float32 [4, 128], replicated, may hold values from -1 to 1
- dest_lane: int32 [65536], P(('grp', 'lane')), may hold values from 0 to 3, as said below
- dest_slot: int32 [65536], P(('grp', 'lane')), may hold values from 0 to 2047, as said below
Outputs:
- table_out: bfloat16 [65536, 128], P(('grp', 'lane'))
Inputs may be any that keep to these rules, and one draw needn't show every extreme that they name: `send_count`: in every draw for each of the two directions some partition has exactly 512 live rows towards that neighbour. `dest_lane`: within each relayout group every row of every table shard is named by exactly one node; at most 1024 rows of one partition go to one shard, and exactly 1024 for some pair in every group. `dest_slot`: together with dest_lane, a one-to-one map of a group's nodes onto its table rows.
All inputs are finite; a program needn't handle non-finite values.
Results may differ from a plain program's by a relative error of at most 0.008.
Values may be sent and summed in bfloat16 or wider, within the bound.
A program may use at most 64 MiB of HBM per device.

v0:
```python
import jax
import jax.numpy as jnp
from jax import lax
from jax.sharding import PartitionSpec as P

ORDER = 3


def from_behind(value, axis, by):
    devices = lax.axis_size(axis)
    return lax.ppermute(value, axis, [(i, (i + by) % devices) for i in range(devices)])


def to_ball(white, feature_width):
    norms = jnp.sqrt(jnp.sum(white * white, axis=1, keepdims=True) + 1e-06)
    radius = jnp.sqrt(jnp.float32(feature_width))
    return (jnp.tanh(norms / radius) * radius * white / norms).astype(jnp.bfloat16)


def whiten(values, factor, node_total):
    solved = jax.scipy.linalg.solve_triangular(factor, values.T, lower=True).T
    return solved * jnp.sqrt(jnp.float32(node_total))


def pack_rows(values, destination, slot_ids, lanes, capacity):
    row_count = values.shape[0]
    onehot = (destination[:, None] == jnp.arange(lanes)[None, :]).astype(jnp.int32)
    rank_in_run = jnp.sum(jnp.cumsum(onehot, axis=0) * onehot, axis=1) - 1
    position = destination * capacity + rank_in_run
    buffer = jnp.zeros((lanes * capacity, values.shape[1]), values.dtype).at[position].set(values)
    slot_buffer = jnp.full((lanes * capacity,), row_count, jnp.int32).at[position].set(slot_ids)
    return (buffer.reshape(lanes, capacity, values.shape[1]), slot_buffer.reshape(lanes, capacity))


def place_rows(received, received_slots, row_count):
    flat_slots = received_slots.reshape(-1)
    empty = jnp.zeros((row_count, received.shape[-1]), jnp.bfloat16)
    return empty.at[flat_slots].set(received, mode="drop")


def body(features, tiles, tile_cols, send_index, send_count, coef, dest_lane, dest_slot):
    row_count, feature_width = features.shape
    tile_size = tiles.shape[2]
    lanes = lax.axis_size("lane")
    node_total = row_count * lax.axis_size("grp") * lanes
    capacity = 2 * row_count // lanes
    boundary = send_index.shape[2]
    valid_rows = jnp.arange(boundary)[None, :] < send_count[0][:, None]

    def operate(current):
        upward = jnp.where(
            valid_rows[0][:, None], current[send_index[0, 0]], jnp.zeros((), jnp.bfloat16)
        )
        downward = jnp.where(
            valid_rows[1][:, None], current[send_index[0, 1]], jnp.zeros((), jnp.bfloat16)
        )
        from_lower = from_behind(upward, "grp", 1)
        from_upper = from_behind(downward, "grp", -1)
        extended = jnp.concatenate([current, from_lower, from_upper], axis=0).reshape(
            -1, tile_size, feature_width
        )
        blocks = extended[tile_cols]
        product = jnp.einsum("bkij,bkjf->bif", tiles, blocks, preferred_element_type=jnp.float32)
        return product.reshape(row_count, feature_width)

    def next_term(cheb_terms):
        if len(cheb_terms) == 1:
            return operate(cheb_terms[0]).astype(jnp.bfloat16)
        return (2.0 * operate(cheb_terms[-1]) - cheb_terms[-2].astype(jnp.float32)).astype(
            jnp.bfloat16
        )

    cheb_terms = [features]
    for term_order in range(1, ORDER):
        cheb_terms.append(next_term(cheb_terms))
    cheb_terms.append(next_term(cheb_terms))
    mixed = jnp.zeros((row_count, feature_width), jnp.float32)
    for term_order in range(ORDER + 1):
        mixed = mixed + coef[term_order][None, :] * cheb_terms[term_order].astype(jnp.float32)
    raw_buffer, raw_slots = pack_rows(mixed, dest_lane, dest_slot, lanes, capacity)
    received_raw, received_slots = (
        lax.all_to_all(raw_buffer, "lane", split_axis=0, concat_axis=0, tiled=True),
        lax.all_to_all(raw_slots, "lane", split_axis=0, concat_axis=0, tiled=True),
    )
    local_gram = jnp.einsum("rf,rg->fg", mixed, mixed, precision=lax.Precision.HIGHEST)
    gram = lax.psum(local_gram, ("grp", "lane"))
    factor = jnp.linalg.cholesky(gram)
    flat_raw = received_raw.reshape(-1, feature_width)
    ball_rows = to_ball(whiten(flat_raw, factor, node_total), feature_width)
    return place_rows(ball_rows, received_slots, row_count)


def solution(mesh):
    placed = (
        P(("grp", "lane"), None),
        P(("grp", "lane"), None, None, None),
        P(("grp", "lane"), None),
        P(("grp", "lane"), None, None),
        P(("grp", "lane"), None),
        P(),
        P(("grp", "lane")),
        P(("grp", "lane")),
    )
    return jax.shard_map(
        body, mesh=mesh, in_specs=placed, out_specs=P(("grp", "lane"), None), check_vma=False
    )
```

profile of v0, /device:TPU:1, one launch (start us, length us, event | category | flops | bytes accessed | tf_op | source)
XLA Modules:
  0.0 245.4 jit_solution(8330663186755694221)
XLA Ops:
  6.5 0.8 compare_select_fusion.3
  7.3 0.7 iota_compare_fusion.4
  8.1 2.2 gather_fusion
  10.2 0.1 broadcast_select_fusion.5
  10.4 2.1 collective-permute-start
  12.5 1.3 gather_fusion.1
  13.8 0.1 broadcast_select_fusion.2
  14.0 3.1 %collective-permute-start.1 = (bf16[512,128]{1,0:T(8,128)(2,1)S(1)}, bf16[512,128]{1,0:T(8,128)(2,1)S(1)}, u32[]{:S(2)}, u32[]{:S(2)}) collective-permute-start(bf16[512,128]{1,0:T(8,128)(2,1)S(1)} %broadcast_select_fusion.2), channel_id=1, source_target_pairs={{0,28},{4,0},{8,4},{12,8},{16,12},{20,16},{24,20},{28,24},{1,29},{... | collective-permute-start | bytes 393224 | tf_op jit(solution)/shard_map/ppermute | solution.py:11
  17.2 0.1 reshape.183
  17.3 1.2 reduce-window.6
  18.5 0.2 slice_reduce_fusion
  18.7 0.2 reduce-window.9
  19.0 3.2 %collective-permute-done.1 = bf16[512,128]{1,0:T(8,128)(2,1)S(1)} collective-permute-done((bf16[512,128]{1,0:T(8,128)(2,1)S(1)}, bf16[512,128]{1,0:T(8,128)(2,1)S(1)}, u32[]{:S(2)}, u32[]{:S(2)}) %collective-permute-start.1) | collective-permute-done | bytes 131104 | tf_op jit(solution)/shard_map/ppermute | solution.py:11
  22.3 2.9 %gather_fusion.2 = bf16[112,128,128]{2,1,0:T(8,128)(2,1)} fusion(bf16[24,128,128]{2,1,0:T(8,128)(2,1)S(1)} %bitcast.98, s32[1024]{0:T(1024)S(1)} %pad_clamp_fusion), kind=kCustom, calls=%fused_computation.2 | custom fusion | bytes 7340480 | tf_op jit(solution)/shard_map/gather | solution.py:62
  25.2 4.3 %fusion.2 = bf16[16,128,128]{1,2,0:T(8,128)(2,1)S(1)} fusion(bf16[16,7,128,128]{3,2,1,0:T(8,128)(2,1)} %param.9, bf16[16,7,128,128]{3,2,1,0:T(8,128)(2,1)} %bitcast.94), kind=kOutput, calls=%fused_computation.23 | convolution fusion | flops 470024192 | bytes 7864320 | tf_op jit(solution)/shard_map/bkij,bkjf->bif/dot_general | solution.py:63
  29.4 1.3 gather_fusion.3
  30.8 1.3 gather_fusion.4
  32.1 0.1 broadcast_select_fusion.4
  32.3 0.1 broadcast_select_fusion.1
  32.5 4.2 %collective-permute-start.3 = (bf16[512,128]{1,0:T(8,128)(2,1)S(1)}, bf16[512,128]{1,0:T(8,128)(2,1)S(1)}, u32[]{:S(2)}, u32[]{:S(2)}) collective-permute-start(bf16[512,128]{1,0:T(8,128)(2,1)S(1)} %broadcast_select_fusion.1), channel_id=1, source_target_pairs={{0,28},{4,0},{8,4},{12,8},{16,12},{20,16},{24,20},{28,24},{1,29},{... | collective-permute-start | bytes 393224 | tf_op jit(solution)/shard_map/ppermute | solution.py:11
  36.7 8.8 %scatter_custom_fusion = s32[4096]{0:T(1024)} fusion(s32[2048]{0:T(1024)S(1)} %compare_select_fusion.1, s32[2048]{0:T(1024)} %param.15, s32[]{:T(128)} %constant.66.clone.1), kind=kCustom, calls=%fused_computation.66 | custom fusion | bytes 16896 | tf_op jit(solution)/shard_map/scatter | solution.py:31
  45.5 4.3 %all-to-all-start = ((s32[4,1,1024]{2,1,0:T(1,128)}), s32[4,1,1024]{2,1,0:T(1,128)S(1)}, u32[]{:S(2)}, u32[]{:S(2)}) async-start(s32[4,1,1024]{2,1,0:T(1,128)} %bitcast.2), calls=%async_computation | async-start | bytes 32768 | tf_op jit(solution)/shard_map/all_to_all | solution.py:83
  49.8 2.9 %gather_fusion.5 = bf16[112,128,128]{2,1,0:T(8,128)(2,1)} fusion(bf16[24,128,128]{2,1,0:T(8,128)(2,1)S(1)} %bitcast.99, s32[1024]{0:T(1024)S(1)} %pad_clamp_fusion), kind=kCustom, calls=%fused_computation.5 | custom fusion | bytes 7340480 | tf_op jit(solution)/shard_map/gather | solution.py:62
  52.7 4.3 %fusion = f32[16,128,128]{1,2,0:T(8,128)S(1)} fusion(bf16[16,7,128,128]{3,2,1,0:T(8,128)(2,1)} %param.9, bf16[16,7,128,128]{3,2,1,0:T(8,128)(2,1)} %bitcast.96), kind=kOutput, calls=%fused_computation.17 | convolution fusion | flops 470024192 | bytes 8388608 | tf_op jit(solution)/shard_map/bkij,bkjf->bif/dot_general | solution.py:63
  57.0 0.1 fusion.6
  57.1 1.3 gather_fusion.6
  58.5 1.3 gather_fusion.7
  59.8 0.1 broadcast_select_fusion.3
  60.0 0.1 broadcast_select_fusion
  60.2 4.4 %collective-permute-start.5 = (bf16[512,128]{1,0:T(8,128)(2,1)S(1)}, bf16[512,128]{1,0:T(8,128)(2,1)S(1)}, u32[]{:S(2)}, u32[]{:S(2)}) collective-permute-start(bf16[512,128]{1,0:T(8,128)(2,1)S(1)} %broadcast_select_fusion), channel_id=1, source_target_pairs={{0,28},{4,0},{8,4},{12,8},{16,12},{20,16},{24,20},{28,24},{1,29},{... | collective-permute-start | bytes 393224 | tf_op jit(solution)/shard_map/ppermute | solution.py:11
  64.6 3.2 %collective-permute-done.4 = bf16[512,128]{1,0:T(8,128)(2,1)S(1)} collective-permute-done((bf16[512,128]{1,0:T(8,128)(2,1)S(1)}, bf16[512,128]{1,0:T(8,128)(2,1)S(1)}, u32[]{:S(2)}, u32[]{:S(2)}) %collective-permute-start.4) | collective-permute-done | bytes 131104 | tf_op jit(solution)/shard_map/ppermute | solution.py:11
  67.8 2.9 %gather_fusion.8 = bf16[112,128,128]{2,1,0:T(8,128)(2,1)} fusion(bf16[24,128,128]{2,1,0:T(8,128)(2,1)S(1)} %bitcast.97, s32[1024]{0:T(1024)S(1)} %pad_clamp_fusion), kind=kCustom, calls=%fused_computation.8 | custom fusion | bytes 7340480 | tf_op jit(solution)/shard_map/gather | solution.py:62
  70.7 4.3 %fusion.1 = f32[16,128,128]{1,2,0:T(8,128)S(1)} fusion(bf16[16,7,128,128]{3,2,1,0:T(8,128)(2,1)} %param.9, bf16[16,7,128,128]{3,2,1,0:T(8,128)(2,1)} %bitcast.95), kind=kOutput, calls=%fused_computation.18 | convolution fusion | flops 470024192 | bytes 8388608 | tf_op jit(solution)/shard_map/bkij,bkjf->bif/dot_general | solution.py:63
  74.9 0.4 fusion.5
  75.4 2.4 fusion.21
  77.9 7.0 %scatter_custom_fusion.1 = f32[4096,128]{1,0:T(8,128)} fusion(s32[2048]{0:T(1024)S(1)} %compare_select_fusion.1, f32[2048,128]{1,0:T(8,128)S(1)} %fusion.5, f32[]{:T(128)} %constant.71.clone.1), kind=kCustom, calls=%fused_computation.29 | custom fusion | bytes 2097156 | tf_op jit(solution)/shard_map/scatter | solution.py:30
  84.9 4.9 %all-to-all-start.1 = ((f32[4,1024,128]{2,1,0:T(8,128)}), f32[4,1024,128]{2,1,0:T(8,128)S(1)}, u32[]{:S(2)}, u32[]{:S(2)}) async-start(f32[4,1024,128]{2,1,0:T(8,128)} %bitcast.100), calls=%async_computation.1 | async-start | bytes 4194304 | tf_op jit(solution)/shard_map/all_to_all | solution.py:82
  89.9 109.3 %all-reduce.2.cloned.1.call-done = f32[128,128]{0,1:T(8,128)} async-done(((f32[128,128]{0,1:T(8,128)}), f32[128,128]{0,1:T(8,128)}) %all-reduce.2.cloned.1.call-update) | async-done | bytes 65552 | tf_op jit(solution)/shard_map/psum | solution.py:86
  199.2 0.9 copy.14
  200.1 0.9 fusion.15
  201.0 11.7 %cholesky.16 = f32[128,128]{1,0:T(8,128)S(1)} custom-call(f32[128,128]{1,0:T(8,128)S(1)} %fusion.15), custom_call_target="Cholesky" | custom-call | tf_op jit(solution)/shard_map/jit(cholesky)/cholesky | solution.py:87
  212.7 0.6 compare_reduce_fusion
  213.4 0.7 fusion.12
  214.1 9.8 %custom-call.7 = f32[1,128,128]{1,2,0:T(8,128)S(1)} custom-call(f32[1,128,128]{2,1,0:T(8,128)S(1)} %fusion.12), custom_call_target="InvertDiagBlocksLowerTriangular" | custom-call | tf_op jit(solution)/shard_map/jit(_solve_triangular)/triangular_solve | solution.py:21
  223.9 2.2 multiply_reduce_fusion
  226.1 0.2 divide_convert_fusion
  226.3 0.7 copy.15
  227.0 11.6 %scatter_custom_fusion.2 = bf16[2048,128]{1,0:T(8,128)(2,1)} fusion(s32[4096]{0:T(1024)S(1)} %bitcast.104, bf16[4096,128]{1,0:T(8,128)(2,1)S(1)} %copy.15, bf16[]{:T(256)} %constant.65.clone.1), kind=kCustom, calls=%fused_computation.34 | custom fusion | bytes 524290 | tf_op jit(solution)/shard_map/scatter | solution.py:38
  (35 shorter events, 0.7 us)
Async XLA Ops:
  6.5 6.0 %copy-start = (bf16[2048,128]{1,0:T(8,128)(2,1)S(1)}, bf16[2048,128]{1,0:T(8,128)(2,1)}, u32[]{:S(2)}) copy-start(bf16[2048,128]{1,0:T(8,128)(2,1)} %param.8) | copy-start | bytes 1572868
  6.5 10.6 %copy-start.2 = (s32[16,7]{0,1:T(8,128)S(1)}, s32[16,7]{0,1:T(8,128)}, u32[]{:S(2)}) copy-start(s32[16,7]{0,1:T(8,128)} %param.10) | copy-start | bytes 1348
  6.5 10.8 %copy-start.1 = (s32[2048]{0:T(1024)S(1)}, s32[2048]{0:T(1024)}, u32[]{:S(2)}) copy-start(s32[2048]{0:T(1024)} %param.14) | copy-start | bytes 24580
  10.4 8.6 %collective-permute-start = (bf16[512,128]{1,0:T(8,128)(2,1)S(1)}, bf16[512,128]{1,0:T(8,128)(2,1)S(1)}, u32[]{:S(2)}, u32[]{:S(2)}) collective-permute-start(bf16[512,128]{1,0:T(8,128)(2,1)S(1)} %broadcast_select_fusion.5), channel_id=1, source_target_pairs={{0,4},{4,8},{8,12},{12,16},{16,20},{20,24},{24,28},{28,0},{1,5},{5... | collective-permute-start | bytes 393224 | tf_op jit(solution)/shard_map/ppermute | solution.py:11
  14.0 8.3 %collective-permute-start.1 = (bf16[512,128]{1,0:T(8,128)(2,1)S(1)}, bf16[512,128]{1,0:T(8,128)(2,1)S(1)}, u32[]{:S(2)}, u32[]{:S(2)}) collective-permute-start(bf16[512,128]{1,0:T(8,128)(2,1)S(1)} %broadcast_select_fusion.2), channel_id=1, source_target_pairs={{0,28},{4,0},{8,4},{12,8},{16,12},{20,16},{24,20},{28,24},{1,29},{... | collective-permute-start | bytes 393224 | tf_op jit(solution)/shard_map/ppermute | solution.py:11
  32.3 17.5 %collective-permute-start.2 = (bf16[512,128]{1,0:T(8,128)(2,1)S(1)}, bf16[512,128]{1,0:T(8,128)(2,1)S(1)}, u32[]{:S(2)}, u32[]{:S(2)}) collective-permute-start(bf16[512,128]{1,0:T(8,128)(2,1)S(1)} %broadcast_select_fusion.4), channel_id=1, source_target_pairs={{0,4},{4,8},{8,12},{12,16},{16,20},{20,24},{24,28},{28,0},{1,5},{5... | collective-permute-start | bytes 393224 | tf_op jit(solution)/shard_map/ppermute | solution.py:11
  32.5 17.3 %collective-permute-start.3 = (bf16[512,128]{1,0:T(8,128)(2,1)S(1)}, bf16[512,128]{1,0:T(8,128)(2,1)S(1)}, u32[]{:S(2)}, u32[]{:S(2)}) collective-permute-start(bf16[512,128]{1,0:T(8,128)(2,1)S(1)} %broadcast_select_fusion.1), channel_id=1, source_target_pairs={{0,28},{4,0},{8,4},{12,8},{16,12},{20,16},{24,20},{28,24},{1,29},{... | collective-permute-start | bytes 393224 | tf_op jit(solution)/shard_map/ppermute | solution.py:11
  45.5 39.4 %all-to-all-start = ((s32[4,1,1024]{2,1,0:T(1,128)}), s32[4,1,1024]{2,1,0:T(1,128)S(1)}, u32[]{:S(2)}, u32[]{:S(2)}) async-start(s32[4,1,1024]{2,1,0:T(1,128)} %bitcast.2), calls=%async_computation | async-start | bytes 32768 | tf_op jit(solution)/shard_map/all_to_all | solution.py:83
  49.8 149.5 %all-reduce.2.cloned.1.call-start = ((), (), s32[]{:S(2)}) async-start(), calls=%async_computation.2 | async-start | bytes 131072 | tf_op jit(solution)/shard_map/psum | solution.py:86
  57.0 7.6 %copy-start.3 = (f32[4,128]{1,0:T(4,128)S(1)}, f32[4,128]{1,0:T(4,128)}, u32[]{:S(2)}) copy-start(f32[4,128]{1,0:T(4,128)} %param.13) | copy-start | bytes 6148
  59.9 7.8 %collective-permute-start.4 = (bf16[512,128]{1,0:T(8,128)(2,1)S(1)}, bf16[512,128]{1,0:T(8,128)(2,1)S(1)}, u32[]{:S(2)}, u32[]{:S(2)}) collective-permute-start(bf16[512,128]{1,0:T(8,128)(2,1)S(1)} %broadcast_select_fusion.3), channel_id=1, source_target_pairs={{0,4},{4,8},{8,12},{12,16},{16,20},{20,24},{24,28},{28,0},{1,5},{5... | collective-permute-start | bytes 393224 | tf_op jit(solution)/shard_map/ppermute | solution.py:11
  60.2 7.6 %collective-permute-start.5 = (bf16[512,128]{1,0:T(8,128)(2,1)S(1)}, bf16[512,128]{1,0:T(8,128)(2,1)S(1)}, u32[]{:S(2)}, u32[]{:S(2)}) collective-permute-start(bf16[512,128]{1,0:T(8,128)(2,1)S(1)} %broadcast_select_fusion), channel_id=1, source_target_pairs={{0,28},{4,0},{8,4},{12,8},{16,12},{20,16},{24,20},{28,24},{1,29},{... | collective-permute-start | bytes 393224 | tf_op jit(solution)/shard_map/ppermute | solution.py:11
  84.9 139.0 %all-to-all-start.1 = ((f32[4,1024,128]{2,1,0:T(8,128)}), f32[4,1024,128]{2,1,0:T(8,128)S(1)}, u32[]{:S(2)}, u32[]{:S(2)}) async-start(f32[4,1024,128]{2,1,0:T(8,128)} %bitcast.100), calls=%async_computation.1 | async-start | bytes 4194304 | tf_op jit(solution)/shard_map/all_to_all | solution.py:82
Sparse Core Ops, SparseCore 0:
  78.0 121.1 all-reduce.1
where the time goes:
time: 246 us; the launch traced here: 245 us
  waiting for transfers between devices  116 us (47%)
  local copies, waits for them, and re-layouts  46.9 us (19%)
  other arithmetic  28.5 us (12%)
  starting transfers between devices  23.2 us (9%)
  matrix products  17.4 us (7%)
  between operations  13.7 us (6%)
    psum x1, waiting for transfers between devices, body(): gram = lax.psum(local_gram, ('grp', 'lane'))  109 us
    ppermute x6, starting transfers between devices, from_behind(): lax.ppermute(value, axis, [(i, (i + by) % devices) for i in range(devices)])  13.9 us
    dot_general x3, matrix products, operate(): jnp.einsum('bkij,bkjf->bif', tiles, blocks, preferred_element_type=jnp.fl...  12.8 us
    another operation x3, other arithmetic, body(): factor = jnp.linalg.cholesky(gram)  12.4 us
    scatter x1, local copies, waits for them, and re-layouts, place_rows(): return empty.at[flat_slots].set(received, mode='drop')  11.6 us
    another operation x2, other arithmetic, whiten(): solved = jax.scipy.linalg.solve_triangular(factor, values.T, lower=True).T  10.5 us
    scatter x1, local copies, waits for them, and re-layouts, pack_rows(): jnp.full((lanes * capacity,), row_count, jnp.int32).at[position]  8.78 us
    gather x3, local copies, waits for them, and re-layouts, operate(): blocks = extended[tile_cols]  8.6 us
  transfers between devices with their start and end apart: 9, of which 3 were waited for; matrix products, arithmetic and copies ran while one was open for 26% of the time, Pallas kernels for 0%

commit v1 on v0

--- a/solution.py
+++ b/solution.py
@@ -1,9 +1,17 @@
+import functools
 import jax
 import jax.numpy as jnp
 from jax import lax
 from jax.sharding import PartitionSpec as P
 
 ORDER = 3
+
+
+def end_the_state(mine_x, shard_axis):
+    return jnp.sum(lax.all_gather(mine_x, shard_axis), axis=0)
+
+
+switch_the_sides = functools.partial(end_the_state, shard_axis=("grp", "lane"))
 
 
 def from_behind(value, axis, by):
@@ -83,7 +91,7 @@
         lax.all_to_all(raw_slots, "lane", split_axis=0, concat_axis=0, tiled=True),
     )
     local_gram = jnp.einsum("rf,rg->fg", mixed, mixed, precision=lax.Precision.HIGHEST)
-    gram = lax.psum(local_gram, ("grp", "lane"))
+    gram = switch_the_sides(local_gram)
     factor = jnp.linalg.cholesky(gram)
     flat_raw = received_raw.reshape(-1, feature_width)
     ball_rows = to_ball(whiten(flat_raw, factor, node_total), feature_width)

time: 246 us -> 177 us (0.72)
  waiting for transfers between devices: 116 us -> 45.8 us
    psum x1 -> x0, waiting for transfers between devices: 109 us -> none  [body(): gram = lax.psum(local_gram, ('grp', 'lane'))]
    all_gather x0 -> x1, waiting for transfers between devices: none -> 35.8 us  [end_the_state(): return jnp.sum(lax.all_gather(mine_x, shard_axis), axis=0)]
    ppermute x6, waiting for transfers between devices: 6.42 us -> 9.9 us  [from_behind(): lax.ppermute(value, axis, [(i, (i + by) % devices) for i in range(devices)])]
  transfers between devices with their start and end apart: 9 -> 9, of which waited for: 3 -> 5; matrix products, arithmetic and copies ran while one was open for 26% -> 25% of each run, Pallas kernels for 0% -> 0%
where the time goes in v1:
time: 177 us; the launch traced here: 176 us
  local copies, waits for them, and re-layouts  46 us (26%)
  waiting for transfers between devices  45.8 us (26%)
  other arithmetic  29.4 us (17%)
  starting transfers between devices  24.2 us (14%)
  matrix products  17.4 us (10%)
  between operations  13.7 us (8%)
    all_gather x1, waiting for transfers between devices, end_the_state(): return jnp.sum(lax.all_gather(mine_x, shard_axis), axis=0)  35.8 us
    ppermute x6, starting transfers between devices, from_behind(): lax.ppermute(value, axis, [(i, (i + by) % devices) for i in range(devices)])  13.9 us
    dot_general x3, matrix products, operate(): jnp.einsum('bkij,bkjf->bif', tiles, blocks, preferred_element_type=jnp.fl...  12.8 us
    another operation x3, other arithmetic, body(): factor = jnp.linalg.cholesky(gram)  12.4 us
    scatter x1, local copies, waits for them, and re-layouts, place_rows(): return empty.at[flat_slots].set(received, mode='drop')  11.6 us
    another operation x2, other arithmetic, whiten(): solved = jax.scipy.linalg.solve_triangular(factor, values.T, lower=True).T  10.5 us
    ppermute x6, waiting for transfers between devices, from_behind(): lax.ppermute(value, axis, [(i, (i + by) % devices) for i in range(devices)])  9.9 us
    scatter x1, local copies, waits for them, and re-layouts, pack_rows(): jnp.full((lanes * capacity,), row_count, jnp.int32).at[position]  8.78 us
  transfers between devices with their start and end apart: 9, of which 5 were waited for; matrix products, arithmetic and copies ran while one was open for 25% of the time, Pallas kernels for 0%

profile of v1, /device:TPU:1, one launch (start us, length us, event | category | flops | bytes accessed | tf_op | source)
XLA Modules:
  0.0 176.5 jit_solution(3813342866721215389)
XLA Ops:
  6.5 0.8 compare_select_fusion.3
  7.3 0.7 iota_compare_fusion.4
  8.1 2.2 %gather_fusion = bf16[512,128]{1,0:T(8,128)(2,1)S(1)} fusion(bf16[2048,128]{1,0:T(8,128)(2,1)} %param.8, s32[1024]{0:T(1024)S(1)} %pad_clamp_fusion.2), kind=kCustom, calls=%fused_computation | custom fusion | bytes 264192 | tf_op jit(solution)/shard_map/gather | solution.py:60
  10.2 0.1 broadcast_select_fusion.5
  10.4 2.1 %collective-permute-start = (bf16[512,128]{1,0:T(8,128)(2,1)S(1)}, bf16[512,128]{1,0:T(8,128)(2,1)S(1)}, u32[]{:S(2)}, u32[]{:S(2)}) collective-permute-start(bf16[512,128]{1,0:T(8,128)(2,1)S(1)} %broadcast_select_fusion.5), channel_id=1, source_target_pairs={{0,4},{4,8},{8,12},{12,16},{16,20},{20,24},{24,28},{28,0},{1,5},{5... | collective-permute-start | bytes 393224 | tf_op jit(solution)/shard_map/ppermute | solution.py:19
  12.5 1.3 gather_fusion.1
  13.8 0.1 broadcast_select_fusion.2
  14.0 3.1 %collective-permute-start.1 = (bf16[512,128]{1,0:T(8,128)(2,1)S(1)}, bf16[512,128]{1,0:T(8,128)(2,1)S(1)}, u32[]{:S(2)}, u32[]{:S(2)}) collective-permute-start(bf16[512,128]{1,0:T(8,128)(2,1)S(1)} %broadcast_select_fusion.2), channel_id=1, source_target_pairs={{0,28},{4,0},{8,4},{12,8},{16,12},{20,16},{24,20},{28,24},{1,29},{... | collective-permute-start | bytes 393224 | tf_op jit(solution)/shard_map/ppermute | solution.py:19
  17.3 1.4 collective-permute-done
  18.7 3.5 %collective-permute-done.1 = bf16[512,128]{1,0:T(8,128)(2,1)S(1)} collective-permute-done((bf16[512,128]{1,0:T(8,128)(2,1)S(1)}, bf16[512,128]{1,0:T(8,128)(2,1)S(1)}, u32[]{:S(2)}, u32[]{:S(2)}) %collective-permute-start.1) | collective-permute-done | bytes 131104 | tf_op jit(solution)/shard_map/ppermute | solution.py:19
  22.3 2.9 %gather_fusion.2 = bf16[112,128,128]{2,1,0:T(8,128)(2,1)} fusion(bf16[24,128,128]{2,1,0:T(8,128)(2,1)S(1)} %bitcast.99, s32[1024]{0:T(1024)S(1)} %pad_clamp_fusion), kind=kCustom, calls=%fused_computation.2 | custom fusion | bytes 7340480 | tf_op jit(solution)/shard_map/gather | solution.py:70
  25.2 4.3 %fusion.2 = bf16[16,128,128]{1,2,0:T(8,128)(2,1)S(1)} fusion(bf16[16,7,128,128]{3,2,1,0:T(8,128)(2,1)} %param.9, bf16[16,7,128,128]{3,2,1,0:T(8,128)(2,1)} %bitcast.95), kind=kOutput, calls=%fused_computation.23 | convolution fusion | flops 470024192 | bytes 7864320 | tf_op jit(solution)/shard_map/bkij,bkjf->bif/dot_general | solution.py:71
  29.4 1.3 gather_fusion.3
  30.8 1.3 gather_fusion.4
  32.1 0.1 broadcast_select_fusion.4
  32.3 0.1 broadcast_select_fusion.1
  32.5 4.2 %collective-permute-start.3 = (bf16[512,128]{1,0:T(8,128)(2,1)S(1)}, bf16[512,128]{1,0:T(8,128)(2,1)S(1)}, u32[]{:S(2)}, u32[]{:S(2)}) collective-permute-start(bf16[512,128]{1,0:T(8,128)(2,1)S(1)} %broadcast_select_fusion.1), channel_id=1, source_target_pairs={{0,28},{4,0},{8,4},{12,8},{16,12},{20,16},{24,20},{28,24},{1,29},{... | collective-permute-start | bytes 393224 | tf_op jit(solution)/shard_map/ppermute | solution.py:19
  36.7 2.9 %collective-permute-done.2 = bf16[512,128]{1,0:T(8,128)(2,1)S(1)} collective-permute-done((bf16[512,128]{1,0:T(8,128)(2,1)S(1)}, bf16[512,128]{1,0:T(8,128)(2,1)S(1)}, u32[]{:S(2)}, u32[]{:S(2)}) %collective-permute-start.2) | collective-permute-done | bytes 131104 | tf_op jit(solution)/shard_map/ppermute | solution.py:19
  39.6 2.9 %gather_fusion.5 = bf16[112,128,128]{2,1,0:T(8,128)(2,1)} fusion(bf16[24,128,128]{2,1,0:T(8,128)(2,1)S(1)} %bitcast.100, s32[1024]{0:T(1024)S(1)} %pad_clamp_fusion), kind=kCustom, calls=%fused_computation.5 | custom fusion | bytes 7340480 | tf_op jit(solution)/shard_map/gather | solution.py:70
  42.5 4.3 %fusion = f32[16,128,128]{1,2,0:T(8,128)S(1)} fusion(bf16[16,7,128,128]{3,2,1,0:T(8,128)(2,1)} %param.9, bf16[16,7,128,128]{3,2,1,0:T(8,128)(2,1)} %bitcast.97), kind=kOutput, calls=%fused_computation.17 | convolution fusion | flops 470024192 | bytes 8388608 | tf_op jit(solution)/shard_map/bkij,bkjf->bif/dot_general | solution.py:71
  46.9 1.3 gather_fusion.6
  48.3 1.3 gather_fusion.7
  49.6 0.1 broadcast_select_fusion.3
  49.7 0.5 collective-permute-start.4
  50.2 0.1 broadcast_select_fusion
  50.4 4.0 %collective-permute-start.5 = (bf16[512,128]{1,0:T(8,128)(2,1)S(1)}, bf16[512,128]{1,0:T(8,128)(2,1)S(1)}, u32[]{:S(2)}, u32[]{:S(2)}) collective-permute-start(bf16[512,128]{1,0:T(8,128)(2,1)S(1)} %broadcast_select_fusion), channel_id=1, source_target_pairs={{0,28},{4,0},{8,4},{12,8},{16,12},{20,16},{24,20},{28,24},{1,29},{... | collective-permute-start | bytes 393224 | tf_op jit(solution)/shard_map/ppermute | solution.py:19
  54.3 2.1 %collective-permute-done.4 = bf16[512,128]{1,0:T(8,128)(2,1)S(1)} collective-permute-done((bf16[512,128]{1,0:T(8,128)(2,1)S(1)}, bf16[512,128]{1,0:T(8,128)(2,1)S(1)}, u32[]{:S(2)}, u32[]{:S(2)}) %collective-permute-start.4) | collective-permute-done | bytes 131104 | tf_op jit(solution)/shard_map/ppermute | solution.py:19
  56.5 2.9 %gather_fusion.8 = bf16[112,128,128]{2,1,0:T(8,128)(2,1)} fusion(bf16[24,128,128]{2,1,0:T(8,128)(2,1)S(1)} %bitcast.98, s32[1024]{0:T(1024)S(1)} %pad_clamp_fusion), kind=kCustom, calls=%fused_computation.8 | custom fusion | bytes 7340480 | tf_op jit(solution)/shard_map/gather | solution.py:70
  59.3 4.3 %fusion.1 = f32[16,128,128]{1,2,0:T(8,128)S(1)} fusion(bf16[16,7,128,128]{3,2,1,0:T(8,128)(2,1)} %param.9, bf16[16,7,128,128]{3,2,1,0:T(8,128)(2,1)} %bitcast.96), kind=kOutput, calls=%fused_computation.18 | convolution fusion | flops 470024192 | bytes 8388608 | tf_op jit(solution)/shard_map/bkij,bkjf->bif/dot_general | solution.py:71
  63.6 0.4 fusion.5
  64.1 2.5 %fusion.21 = f32[128,128]{1,0:T(8,128)} fusion(f32[2048,128]{1,0:T(8,128)S(1)} %fusion.5), kind=kOutput, calls=%fused_computation.79 | convolution fusion | flops 402653184 | bytes 1114112 | tf_op jit(solution)/shard_map/rf,rg->fg/dot_general | solution.py:93
  66.6 1.2 reduce-window.6
  67.7 0.2 slice_reduce_fusion
  68.0 0.2 reduce-window.9
  68.3 8.8 %scatter_custom_fusion = s32[4096]{0:T(1024)} fusion(s32[2048]{0:T(1024)S(1)} %compare_select_fusion.1, s32[2048]{0:T(1024)} %param.15, s32[]{:T(128)} %constant.66.clone.1), kind=kCustom, calls=%fused_computation.66 | custom fusion | bytes 16896 | tf_op jit(solution)/shard_map/scatter | solution.py:39
  77.1 6.5 %all-to-all-start = ((s32[4,1,1024]{2,1,0:T(1,128)}), s32[4,1,1024]{2,1,0:T(1,128)S(1)}, u32[]{:S(2)}, u32[]{:S(2)}) async-start(s32[4,1,1024]{2,1,0:T(1,128)} %bitcast.2), calls=%async_computation | async-start | bytes 32768 | tf_op jit(solution)/shard_map/all_to_all | solution.py:91
  83.6 7.0 %scatter_custom_fusion.1 = f32[4096,128]{1,0:T(8,128)} fusion(s32[2048]{0:T(1024)S(1)} %compare_select_fusion.1, f32[2048,128]{1,0:T(8,128)S(1)} %fusion.5, f32[]{:T(128)} %constant.71.clone.1), kind=kCustom, calls=%fused_computation.29 | custom fusion | bytes 2097156 | tf_op jit(solution)/shard_map/scatter | solution.py:38
  90.5 3.8 %all-to-all-start.1 = ((f32[4,1024,128]{2,1,0:T(8,128)}), f32[4,1024,128]{2,1,0:T(8,128)S(1)}, u32[]{:S(2)}, u32[]{:S(2)}) async-start(f32[4,1024,128]{2,1,0:T(8,128)} %bitcast.101), calls=%async_computation.1 | async-start | bytes 4194304 | tf_op jit(solution)/shard_map/all_to_all | solution.py:90
  94.4 35.8 %all-gather.3.cloned.1.call-done = f32[4096,128]{1,0:T(8,128)} async-done(((f32[128,128]{1,0:T(8,128)}), f32[4096,128]{1,0:T(8,128)}) %all-gather.3.cloned.1.call-update) | async-done | bytes 2097168 | tf_op jit(solution)/shard_map/all_gather | solution.py:11
  130.2 1.7 reduce_sum.28
  132.0 11.7 %cholesky.16 = f32[128,128]{1,0:T(8,128)S(1)} custom-call(f32[128,128]{1,0:T(8,128)S(1)} %fusion.15), custom_call_target="Cholesky" | custom-call | tf_op jit(solution)/shard_map/jit(cholesky)/cholesky | solution.py:95
  143.8 0.6 compare_reduce_fusion
  144.4 0.7 fusion.12
  145.1 9.8 %custom-call.7 = f32[1,128,128]{1,2,0:T(8,128)S(1)} custom-call(f32[1,128,128]{2,1,0:T(8,128)S(1)} %fusion.12), custom_call_target="InvertDiagBlocksLowerTriangular" | custom-call | tf_op jit(solution)/shard_map/jit(_solve_triangular)/triangular_solve | solution.py:29
  154.9 2.2 %multiply_reduce_fusion = (f32[4096]{0:T(1024)S(1)}, f32[4096,128]{0,1:T(8,128)S(1)}) fusion(f32[4096,128]{1,0:T(8,128)S(1)} %bitcast.102, f32[1,128,128]{1,2,0:T(8,128)S(1)} %custom-call.7), kind=kOutput, calls=%fused_computation.13 | convolution fusion | flops 806875136 | bytes 4276224 | tf_op jit(solution)/shard_map/jit(_solve_triangular)/triangular_solve | solution.py:29
  157.1 0.2 divide_convert_fusion
  157.4 0.7 copy.16
  158.0 11.6 %scatter_custom_fusion.2 = bf16[2048,128]{1,0:T(8,128)(2,1)} fusion(s32[4096]{0:T(1024)S(1)} %bitcast.106, bf16[4096,128]{1,0:T(8,128)(2,1)S(1)} %copy.16, bf16[]{:T(256)} %constant.65.clone.1), kind=kCustom, calls=%fused_computation.34 | custom fusion | bytes 524290 | tf_op jit(solution)/shard_map/scatter | solution.py:46
  (36 shorter events, 0.9 us)
Async XLA Ops:
  6.5 6.0 %copy-start = (bf16[2048,128]{1,0:T(8,128)(2,1)S(1)}, bf16[2048,128]{1,0:T(8,128)(2,1)}, u32[]{:S(2)}) copy-start(bf16[2048,128]{1,0:T(8,128)(2,1)} %param.8) | copy-start | bytes 1572868
  6.5 10.6 %copy-start.2 = (s32[16,7]{0,1:T(8,128)S(1)}, s32[16,7]{0,1:T(8,128)}, u32[]{:S(2)}) copy-start(s32[16,7]{0,1:T(8,128)} %param.10) | copy-start | bytes 1348
  6.5 123.7 %all-gather.3.cloned.1.call-start = ((), (), s32[]{:S(2)}) async-start(), calls=%async_computation.2 | async-start | bytes 2162688 | tf_op jit(solution)/shard_map/all_gather | solution.py:11
  10.4 8.4 %collective-permute-start = (bf16[512,128]{1,0:T(8,128)(2,1)S(1)}, bf16[512,128]{1,0:T(8,128)(2,1)S(1)}, u32[]{:S(2)}, u32[]{:S(2)}) collective-permute-start(bf16[512,128]{1,0:T(8,128)(2,1)S(1)} %broadcast_select_fusion.5), channel_id=1, source_target_pairs={{0,4},{4,8},{8,12},{12,16},{16,20},{20,24},{24,28},{28,0},{1,5},{5... | collective-permute-start | bytes 393224 | tf_op jit(solution)/shard_map/ppermute | solution.py:19
  14.0 8.3 %collective-permute-start.1 = (bf16[512,128]{1,0:T(8,128)(2,1)S(1)}, bf16[512,128]{1,0:T(8,128)(2,1)S(1)}, u32[]{:S(2)}, u32[]{:S(2)}) collective-permute-start(bf16[512,128]{1,0:T(8,128)(2,1)S(1)} %broadcast_select_fusion.2), channel_id=1, source_target_pairs={{0,28},{4,0},{8,4},{12,8},{16,12},{20,16},{24,20},{28,24},{1,29},{... | collective-permute-start | bytes 393224 | tf_op jit(solution)/shard_map/ppermute | solution.py:19
  32.3 7.3 %collective-permute-start.2 = (bf16[512,128]{1,0:T(8,128)(2,1)S(1)}, bf16[512,128]{1,0:T(8,128)(2,1)S(1)}, u32[]{:S(2)}, u32[]{:S(2)}) collective-permute-start(bf16[512,128]{1,0:T(8,128)(2,1)S(1)} %broadcast_select_fusion.4), channel_id=1, source_target_pairs={{0,4},{4,8},{8,12},{12,16},{16,20},{20,24},{24,28},{28,0},{1,5},{5... | collective-permute-start | bytes 393224 | tf_op jit(solution)/shard_map/ppermute | solution.py:19
  32.5 7.1 %collective-permute-start.3 = (bf16[512,128]{1,0:T(8,128)(2,1)S(1)}, bf16[512,128]{1,0:T(8,128)(2,1)S(1)}, u32[]{:S(2)}, u32[]{:S(2)}) collective-permute-start(bf16[512,128]{1,0:T(8,128)(2,1)S(1)} %broadcast_select_fusion.1), channel_id=1, source_target_pairs={{0,28},{4,0},{8,4},{12,8},{16,12},{20,16},{24,20},{28,24},{1,29},{... | collective-permute-start | bytes 393224 | tf_op jit(solution)/shard_map/ppermute | solution.py:19
  46.8 7.6 %copy-start.3 = (f32[4,128]{1,0:T(4,128)S(1)}, f32[4,128]{1,0:T(4,128)}, u32[]{:S(2)}) copy-start(f32[4,128]{1,0:T(4,128)} %param.13) | copy-start | bytes 6148
  49.7 6.7 %collective-permute-start.4 = (bf16[512,128]{1,0:T(8,128)(2,1)S(1)}, bf16[512,128]{1,0:T(8,128)(2,1)S(1)}, u32[]{:S(2)}, u32[]{:S(2)}) collective-permute-start(bf16[512,128]{1,0:T(8,128)(2,1)S(1)} %broadcast_select_fusion.3), channel_id=1, source_target_pairs={{0,4},{4,8},{8,12},{12,16},{16,20},{20,24},{24,28},{28,0},{1,5},{5... | collective-permute-start | bytes 393224 | tf_op jit(solution)/shard_map/ppermute | solution.py:19
  50.4 6.1 %collective-permute-start.5 = (bf16[512,128]{1,0:T(8,128)(2,1)S(1)}, bf16[512,128]{1,0:T(8,128)(2,1)S(1)}, u32[]{:S(2)}, u32[]{:S(2)}) collective-permute-start(bf16[512,128]{1,0:T(8,128)(2,1)S(1)} %broadcast_select_fusion), channel_id=1, source_target_pairs={{0,28},{4,0},{8,4},{12,8},{16,12},{20,16},{24,20},{28,24},{1,29},{... | collective-permute-start | bytes 393224 | tf_op jit(solution)/shard_map/ppermute | solution.py:19
  63.6 2.9 %copy-start.1 = (s32[2048]{0:T(1024)S(1)}, s32[2048]{0:T(1024)}, u32[]{:S(2)}) copy-start(s32[2048]{0:T(1024)} %param.14) | copy-start | bytes 24580
  77.1 13.5 %all-to-all-start = ((s32[4,1,1024]{2,1,0:T(1,128)}), s32[4,1,1024]{2,1,0:T(1,128)S(1)}, u32[]{:S(2)}, u32[]{:S(2)}) async-start(s32[4,1,1024]{2,1,0:T(1,128)} %bitcast.2), calls=%async_computation | async-start | bytes 32768 | tf_op jit(solution)/shard_map/all_to_all | solution.py:91
  90.5 64.4 %all-to-all-start.1 = ((f32[4,1024,128]{2,1,0:T(8,128)}), f32[4,1024,128]{2,1,0:T(8,128)S(1)}, u32[]{:S(2)}, u32[]{:S(2)}) async-start(f32[4,1024,128]{2,1,0:T(8,128)} %bitcast.101), calls=%async_computation.1 | async-start | bytes 4194304 | tf_op jit(solution)/shard_map/all_to_all | solution.py:90
Sparse Core Ops, SparseCore 0:
  66.7 63.4 all-gather.2
